TPU v7x, 256 devices: a whole 4x4x8 slice. The times are simulated.
256 devices in a mesh: group: 8 (over y, z_hi), tp: 32 (over x, z_lo, core).
Axes of the slice: x: 4, y: 4, z: 8 (z_hi: 2, z_lo: 4; z = z_hi * 4 + z_lo), core: 2. Of those that a mesh axis runs over, the one named last changes fastest.
Arguments:
- queries: bfloat16 [8, 8, 2, 8192], P('group', None, None, 'tp'), may hold values from -24 to 24
- new_keys: bfloat16 [8, 8, 2, 1024], P('group', None, None, 'tp'), may hold values from -16 to 16
- new_values: bfloat16 [8, 8, 2, 1024], P('group', None, None, 'tp'), may hold values from -24 to 24
- key_pages: bfloat16 [8, 2048, 16, 1024], P('group', 'tp'), may hold values from -16 to 16
- value_pages: bfloat16 [8, 2048, 16, 1024], P('group', 'tp'), may hold values from -24 to 24
- page_owner: int32 [8, 2048], P('group', 'tp'), may hold values from 0 to 8, as said below
- page_fill: int32 [8, 2048], P('group', 'tp'), may hold values from 0 to 16, as said below
- target_slot: int32 [8, 8], P('group'), may hold values from 0 to 8, as said below
- out_weight: bfloat16 [8192, 8192], P(None, 'tp'), may hold values from -0.0625 to 0.0625
Outputs:
- projected: bfloat16 [8, 8, 2, 8192], P('group', None, None, 'tp')
Inputs may be any that keep to these rules, and one draw needn't show every extreme that they name: `page_owner`: the owning request slot, or 8 for a free page. Of each pair of groups g and g XOR (4) one is loaded (no free pages) and the other light; group 0 is light, and so is group 8 - 1 when 8 > 2. One device holds at most 16 pages of moving requests, and some device of every loaded group holds exactly 16. `page_fill`: 1 to 16 for a used page, 0 for a free one. `target_slot`: 8 for a request that stays. Every group has exactly one moving request; their slots in the partner group are distinct and own no pages there.
All inputs are finite; a program needn't handle non-finite values.
Results may differ from a plain program's by a relative error of at most 0.0065.
Values may be sent and summed in bfloat16 or wider, within the bound.
A program may use at most 64 MiB of HBM per device.

v0:
```python
import math
import jax
import jax.numpy as jnp
from jax import lax
from jax.sharding import PartitionSpec as P

HEADS = 64
KVH = 8
HD = 128
PAGE = 16
MOVE = 1
neg_big = -1e30


def side_by_side(arrays, axis, dim, along):
    ends, at = ([], 0)
    for a in arrays[:-1]:
        at += a.shape[along]
        ends.append(at)
    both = jnp.concatenate(arrays, axis=along)
    return tuple(jnp.split(lax.all_gather(both, axis, axis=dim, tiled=True), ends, axis=along))


def swapped(value, axis, distance):
    return lax.ppermute(value, axis, [(i, i ^ 1 << distance) for i in range(lax.axis_size(axis))])


def copy_for_each(value, axis):
    peers = lax.axis_size(axis)
    return lax.all_to_all(
        jnp.broadcast_to(value[None], (peers, *value.shape)), axis, 0, 0, tiled=True
    )


def taken_together(value, axis):
    return copy_for_each(value, axis).max(axis=0)


def split_up(value, dim, peers):
    before, after = (value.shape[:dim], value.shape[dim + 1 :])
    return jnp.moveaxis(value.reshape(*before, peers, -1, *after), dim, 0)


def summed_on_arrival(value, axis, dim):
    blocks = split_up(value, dim, lax.axis_size(axis))
    arrived = lax.all_to_all(blocks, axis, split_axis=0, concat_axis=0, tiled=True)
    return arrived.sum(axis=0)


def in_one_piece(arrays, axis, dim, along):
    columns = [a.reshape(*a.shape[:along], -1) for a in arrays]
    both = jnp.concatenate(columns, axis=along)
    out, at, finished = (summed_on_arrival(both, axis, dim), 0, [])
    for a, column in zip(arrays, columns):
        share = out[..., at : at + column.shape[along]]
        finished.append(share.reshape(*share.shape[:along], *a.shape[along:]))
        at += column.shape[along]
    return tuple(finished)


def laid_out(blocks, dim):
    blocks = jnp.moveaxis(blocks, 0, dim)
    shape = blocks.shape
    return blocks.reshape(*shape[:dim], shape[dim] * shape[dim + 1], *shape[dim + 2 :])


def collect(value, axis, dim):
    return laid_out(copy_for_each(value, axis), dim)


def merge_states(first, second):
    largest = jnp.maximum(first[0], second[0])
    scale_first = jnp.exp(first[0] - largest)
    scale_second = jnp.exp(second[0] - largest)
    return (
        largest,
        first[1] * scale_first + second[1] * scale_second,
        first[2] * scale_first[..., None] + second[2] * scale_second[..., None],
    )


def page_states(query_rows, key_block, value_block, owner_rows, fill_counts, row_count):
    page_count = key_block.shape[0]
    step_count = query_rows.shape[1]
    group_size = HEADS // KVH
    scale_factor = 1.0 / math.sqrt(HD)
    clipped = jnp.clip(owner_rows, 0, row_count - 1)
    query_page = jnp.take(query_rows, clipped, axis=0).reshape(
        page_count, step_count, KVH, group_size, HD
    )
    key_page = key_block.reshape(page_count, PAGE, KVH, HD)
    value_page = value_block.reshape(page_count, PAGE, KVH, HD)
    scores = (
        jnp.einsum("psgjd,ptgd->psgjt", query_page, key_page, preferred_element_type=jnp.float32)
        * scale_factor
    )
    live_token = (owner_rows < row_count)[:, None] & (
        lax.broadcasted_iota(jnp.int32, (page_count, PAGE), 1) < fill_counts[:, None]
    )
    token_mask = live_token[:, None, None, None, :]
    scores = jnp.where(token_mask, scores, neg_big)
    page_top = jnp.max(scores, axis=4).reshape(page_count, step_count * HEADS)
    member = owner_rows[None, :] == lax.broadcasted_iota(jnp.int32, (row_count, page_count), 0)
    row_top = jnp.max(jnp.where(member[:, :, None], page_top[None], neg_big), axis=1)
    top_page = jnp.take(row_top, clipped, axis=0).reshape(
        page_count, step_count, KVH, group_size, 1
    )
    weights = jnp.where(token_mask, jnp.exp(scores - top_page), 0.0).astype(jnp.bfloat16)
    weighted = jnp.einsum(
        "psgjt,ptgd->psgjd", weights, value_page, preferred_element_type=jnp.float32
    ).reshape(page_count, step_count * HEADS * HD)
    weight_sum = jnp.sum(weights.astype(jnp.float32), axis=4).reshape(
        page_count, step_count * HEADS
    )
    onehot = member.astype(jnp.float32)
    row_sum = jnp.dot(onehot, weight_sum)
    row_acc = jnp.dot(onehot, weighted)
    return (
        row_top.reshape(row_count, step_count, HEADS),
        row_sum.reshape(row_count, step_count, HEADS),
        row_acc.reshape(row_count, step_count, HEADS, HD),
    )


def new_token_states(query_heads, key_rows, value_rows, head_kv):
    row_count = key_rows.shape[0]
    step_count = key_rows.shape[1]
    scale_factor = 1.0 / math.sqrt(HD)
    key_heads = jnp.take(key_rows.reshape(row_count, step_count, KVH, HD), head_kv, axis=2)
    value_heads = jnp.take(
        value_rows.reshape(row_count, step_count, KVH, HD), head_kv, axis=2
    ).astype(jnp.float32)
    scores = (
        jnp.einsum("rshd,ruhd->rshu", query_heads, key_heads, preferred_element_type=jnp.float32)
        * scale_factor
    )
    causal = (
        lax.broadcasted_iota(jnp.int32, (step_count, step_count), 1)
        <= lax.broadcasted_iota(jnp.int32, (step_count, step_count), 0)
    )[None, :, None, :]
    scores = jnp.where(causal, scores, neg_big)
    largest = jnp.max(scores, axis=3)
    weights = jnp.where(causal, jnp.exp(scores - largest[..., None]), 0.0)
    return (largest, jnp.sum(weights, axis=3), jnp.einsum("rshu,ruhd->rshd", weights, value_heads))


def per_device(
    queries,
    new_keys,
    new_values,
    key_pages,
    value_pages,
    page_owner,
    page_fill,
    target_slot,
    out_weight,
):
    row_count = queries.shape[1]
    step_count = queries.shape[2]
    partner_bit = lax.axis_size("group").bit_length() - 2
    query_rows, key_rows, value_rows = (
        lax.all_gather(queries[0], "tp", axis=2, tiled=True),
        *side_by_side((new_keys[0], new_values[0]), "tp", 2, 0),
    )
    owners = page_owner[0]
    fill_counts = page_fill[0]
    slot_targets = target_slot[0]
    clipped = jnp.clip(owners, 0, row_count - 1)
    page_target = jnp.take(slot_targets, clipped)
    occupied = owners < row_count
    moving = occupied & (page_target < row_count)
    partner_targets = swapped(slot_targets, "group", partner_bit)
    slot_ids = lax.broadcasted_iota(jnp.int32, (row_count,), 0)
    mover_ids = lax.broadcasted_iota(jnp.int32, (MOVE, row_count), 0)
    their_moving = partner_targets < row_count
    their_rank = jnp.cumsum(their_moving.astype(jnp.int32)) - 1
    their_pick = their_moving[None, :] & (their_rank[None, :] == mover_ids)
    pick_rows = jnp.sum(their_pick.astype(jnp.int32) * partner_targets[None, :], axis=1)
    pick_valid = jnp.any(their_pick, axis=1)
    send_pick = pick_valid[:, None] & (pick_rows[:, None] == slot_ids[None, :])
    sent_queries = jnp.einsum(
        "mr,rsd->msd",
        send_pick.astype(jnp.bfloat16),
        query_rows,
        preferred_element_type=jnp.float32,
    ).astype(jnp.bfloat16)
    arrived_queries = swapped(sent_queries, "group", partner_bit)
    own_moving = slot_targets < row_count
    own_rank = jnp.cumsum(own_moving.astype(jnp.int32)) - 1
    page_rank = jnp.take(own_rank, clipped)
    local_rows = jnp.where(
        occupied, jnp.where(moving, row_count + page_rank, owners), row_count + MOVE
    )
    joined = page_states(
        jnp.concatenate([query_rows, arrived_queries], axis=0),
        key_pages[0],
        value_pages[0],
        local_rows,
        fill_counts,
        row_count + MOVE,
    )
    own_part = tuple((member_array[:row_count] for member_array in joined))
    theirs = tuple((member_array[row_count:] for member_array in joined))
    returned = swapped((theirs[0], theirs[1], theirs[2]), "group", partner_bit)
    placement_table = send_pick.astype(jnp.float32)
    placed_any = jnp.any(send_pick, axis=0)
    placed_max = jnp.where(
        placed_any[:, None, None], jnp.einsum("mr,msh->rsh", placement_table, returned[0]), neg_big
    )
    placed_sum = jnp.einsum("mr,msh->rsh", placement_table, returned[1])
    placed_acc = jnp.einsum("mr,mshd->rshd", placement_table, returned[2])
    states = merge_states(own_part, (placed_max, placed_sum, placed_acc))
    head_kv_all = lax.broadcasted_iota(jnp.int32, (HEADS,), 0) // (HEADS // KVH)
    query_heads = query_rows.reshape(row_count, step_count, HEADS, HD)
    largest = taken_together(states[0], "tp")
    shrink = jnp.exp(states[0] - largest)
    share_sum, share_acc = in_one_piece(
        (states[1] * shrink, states[2] * shrink[..., None]), "tp", 2, 3
    )
    share_heads = share_sum.shape[2]
    first_head = lax.axis_index("tp") * share_heads
    share_largest = lax.dynamic_slice_in_dim(largest, first_head, share_heads, 2)
    share_query = lax.dynamic_slice_in_dim(query_heads, first_head, share_heads, 2)
    share_kv = lax.dynamic_slice_in_dim(head_kv_all, first_head, share_heads, 0)
    new_terms = new_token_states(share_query, key_rows, value_rows, share_kv)
    finished = merge_states((share_largest, share_sum, share_acc), new_terms)
    share_attention = (finished[2] / finished[1][..., None]).astype(jnp.bfloat16)
    attention = collect(share_attention, "tp", 2).reshape(row_count * step_count, HEADS * HD)
    projected = jnp.dot(attention, out_weight, preferred_element_type=jnp.float32).astype(
        jnp.bfloat16
    )
    return projected.reshape(1, row_count, step_count, out_weight.shape[1])


def solution(mesh):
    placed = (
        P("group", None, None, "tp"),
        P("group", None, None, "tp"),
        P("group", None, None, "tp"),
        P("group", "tp", None, None),
        P("group", "tp", None, None),
        P("group", "tp"),
        P("group", "tp"),
        P("group", None),
        P(None, "tp"),
    )
    return jax.shard_map(
        per_device,
        mesh=mesh,
        in_specs=placed,
        out_specs=P("group", None, None, "tp"),
        check_vma=False,
    )
```

profile of v0, /device:TPU:1, one launch (start us, length us, event | category | flops | bytes accessed | tf_op | source)
XLA Modules:
  0.0 218.9 jit_solution(16080722643461589940)
XLA Ops:
  0.0 3.7 %collective-permute-start = (s32[8]{0:T(128)}, s32[8]{0:T(128)S(1)}, u32[]{:S(2)}, u32[]{:S(2)}) collective-permute-start(s32[8]{0:T(128)} %bitcast.157), channel_id=1, source_target_pairs={{0,128},{32,160},{64,192},{96,224},{128,0},{160,32},{192,64},{224,... | collective-permute-start | bytes 104 | tf_op jit(solution)/shard_map/ppermute | solution.py:25
  3.7 1.6 fusion.48
  5.4 0.7 fusion.37
  6.0 0.2 reduce-window.18
  6.2 0.7 fusion.49
  6.9 10.6 %broadcast_compare_fusion = (pred[64]{0:T(512)(128)(4,1)S(1)}, s32[64]{0:T(128)S(1)}) fusion(s32[]{:T(128)} %bitcast.19, s32[]{:T(128)} %bitcast.18, s32[]{:T(128)} %bitcast.17, s32[]{:T(128)} %bitcast.16, s32[]{:T(128)} %bitcast.15, s32[]{:T(128)} %bitcast.14, s32[]{:T(128)} %bitcast.13, s32[]{:T(128)} %bitcast.12, s32[]{:T(128)} %bitcast.9, s32[]{:T(128)} %bitcast.8, ...), kind=kLoop, calls=%fused_computation.116 | loop fusion | flops 2368 | bytes 640 | tf_op jit(solution)/shard_map/lt | solution.py:97
  17.5 46.4 %all-gather = bf16[1,8,2,8192]{3,2,1,0:T(2,128)(2,1)S(1)} all-gather(bf16[1,8,2,256]{3,2,1,0:T(2,128)(2,1)} %param.13), channel_id=2, replica_groups=mesh['group'=8,'tp'=32] {'tp'}, dimensions={3}, use_global_device_ids=true | all-gather | bytes 270336 | tf_op jit(solution)/shard_map/all_gather | solution.py:162
  63.9 2.2 %copy.230 = bf16[128,8,8,128]{3,2,1,0:T(8,128)(2,1)S(1)} copy(bf16[128,8,8,128]{3,1,2,0:T(8,128)(2,1)} %bitcast.143) | data formatting | bytes 4194304
  66.2 1.5 bitcast_bitcast_fusion.1
  67.7 0.9 copy-done.1
  68.5 0.6 copy.231
  69.2 1.5 bitcast_bitcast_fusion
  71.0 40.1 %all_gather.7 = bf16[16,2,1024]{0,1,2:T(2,128)(2,1)S(1)} all-gather(bf16[16,2,32]{0,1,2:T(2,128)(2,1)S(1)} %pad_maximum_fusion.1), channel_id=1, replica_groups=mesh['group'=8,'tp'=32] {'tp'}, dimensions={2}, use_global_device_ids=true | all-gather | bytes 67584 | tf_op jit(solution)/shard_map/all_gather | solution.py:21
  111.1 0.2 reduce-window.19
  111.3 0.6 fusion.43
  111.9 0.7 select_reduce_fusion.1
  112.7 1.3 compare_and_fusion.2
  114.0 0.4 fusion.17
  114.5 0.1 collective-permute-start.1
  114.6 1.3 fusion.38
  115.9 2.9 %collective-permute-done.1 = bf16[1,2,8192]{2,1,0:T(2,128)(2,1)S(1)} collective-permute-done((bf16[1,2,8192]{2,1,0:T(2,128)(2,1)S(1)}, bf16[1,2,8192]{2,1,0:T(2,128)(2,1)S(1)}, u32[]{:S(2)}, u32[]{:S(2)}) %collective-permute-start.1) | collective-permute-done | bytes 32800 | tf_op jit(solution)/shard_map/ppermute | solution.py:25
  118.8 0.4 pad_maximum_fusion
  119.2 6.0 %gather_fusion = bf16[64,2,8192]{2,1,0:T(2,128)(2,1)S(1)} fusion(bf16[9,2,8192]{2,1,0:T(2,128)(2,1)S(1)} %pad_maximum_fusion, s32[1024]{0:T(1024)S(1)} %pad_clamp_fusion.1), kind=kCustom, calls=%fused_computation.2 | custom fusion | bytes 4194560 | tf_op jit(solution)/shard_map/jit(_take)/gather | solution.py:88
  125.3 2.9 %gather.19 = bf16[64,2,8,8,128]{4,3,2,1,0:T(8,128)(2,1)} reshape(bf16[64,2,8192]{2,1,0:T(2,128)(2,1)S(1)} %gather_fusion) | data formatting | bytes 4194304 | tf_op jit(solution)/shard_map/jit(_take)/gather | solution.py:88
  128.1 5.8 %bitcast_reduce_fusion = (f32[64,2,8,8]{3,1,2,0:T(2,128)S(1)}, f32[64,8,2,8,16]{4,3,2,1,0:T(8,128)}) fusion(pred[64,16]{1,0:T(8,128)(4,1)S(1)} %fusion.20, bf16[64,16,8,128,1]{3,2,1,0,4:T(8,128)(2,1)} %bitcast_bitcast_fusion.1, bf16[64,2,8,8,128]{4,3,2,1,0:T(8,128)(2,1)} %gather.19, pred[64]{0:T(512)(128)(4,1)S(1)} %get-tuple-element.18), kind=kOutput, calls=%fused_computation.8 | convolution fusion | flops 34988032 | bytes 4752448 | tf_op jit(solution)/shard_map/psgjd,ptgd->psgjt/dot_general | solution.py:94
  133.9 0.3 copy.178
  134.3 0.2 select_reduce_fusion
  134.5 0.6 gather_fusion.1
  135.2 0.3 collective-permute-start.2
  135.6 0.4 copy.181
  136.1 5.7 %convert_reduce_fusion = bf16[64,2,8,8]{3,1,2,0:T(2,128)(2,1)} fusion(f32[64,2,8,8]{3,1,2,0:T(2,128)S(1)} %copy.181, f32[64,8,2,8,16]{4,3,2,1,0:T(8,128)} %get-tuple-element.41, pred[64,16]{1,0:T(8,128)(4,1)S(1)} %fusion.20), kind=kLoop, calls=%fused_computation.12 | loop fusion | flops 909312 | bytes 574464 | tf_op jit(solution)/shard_map/reduce_sum | solution.py:112
  141.8 2.0 convolution_bitcast_fusion
  143.8 0.5 copy.188
  144.4 1.2 fusion
  145.8 0.2 copy.182
  146.1 0.8 reshape.380
  146.9 5.1 %all-to-all-start = ((f32[32,1,1024]{2,1,0:T(1,128)}), f32[32,1,1024]{2,1,0:T(1,128)S(1)}, u32[]{:S(2)}, u32[]{:S(2)}) async-start(f32[32,1,1024]{2,1,0:T(1,128)} %reshape.380), calls=%async_computation | async-start | bytes 262144 | tf_op jit(solution)/shard_map/all_to_all | solution.py:30
  152.4 2.9 %collective-permute-start.3 = (f32[1,2,64]{2,1,0:T(2,128)S(1)}, f32[1,2,64]{2,1,0:T(2,128)S(1)}, u32[]{:S(2)}, u32[]{:S(2)}) collective-permute-start(f32[1,2,64]{2,1,0:T(2,128)S(1)} %slice.49), channel_id=1, source_target_pairs={{0,128},{32,160},{64,192},{96,224},{128,0},{160,32},{192,64},{224,... | collective-permute-start | bytes 1544 | tf_op jit(solution)/shard_map/ppermute | solution.py:25
  155.3 5.5 %all-to-all-done = f32[32,1,1024]{2,1,0:T(1,128)S(1)} async-done(((f32[32,1,1024]{2,1,0:T(1,128)}), f32[32,1,1024]{2,1,0:T(1,128)S(1)}, u32[]{:S(2)}, u32[]{:S(2)}) %all-to-all-start) | async-done | bytes 131104 | tf_op jit(solution)/shard_map/all_to_all | solution.py:30
  160.8 0.5 broadcast.372
  161.3 0.9 reduce.12
  162.9 0.8 copy.192
  163.7 0.5 add_multiply_fusion
  164.2 0.3 maximum_bitcast_fusion
  164.6 1.1 copy.193
  165.7 5.3 %all-to-all-start.1 = ((f32[32,8,2,2,129]{4,1,3,2,0:T(8,128)}), f32[32,8,2,2,129]{4,1,3,2,0:T(8,128)S(1)}, u32[]{:S(2)}, u32[]{:S(2)}) async-start(f32[32,8,2,2,129]{4,1,3,2,0:T(8,128)} %copy.193), calls=%async_computation.1 | async-start | bytes 2097152 | tf_op jit(solution)/shard_map/all_to_all | solution.py:46
  171.0 0.9 fusion.47
  171.9 0.3 copy.199
  172.3 0.3 copy.204
  172.7 0.6 gather_fusion.2
  173.3 0.6 gather_fusion.3
  173.9 0.2 fusion.50
  174.1 0.1 copy.201
  174.4 24.4 %all-to-all-done.1 = f32[32,8,2,2,129]{4,1,3,2,0:T(8,128)S(1)} async-done(((f32[32,8,2,2,129]{4,1,3,2,0:T(8,128)}), f32[32,8,2,2,129]{4,1,3,2,0:T(8,128)S(1)}, u32[]{:S(2)}, u32[]{:S(2)}) %all-to-all-start.1) | async-done | bytes 528416 | tf_op jit(solution)/shard_map/all_to_all | solution.py:46
  199.0 0.2 copy.227
  199.3 0.1 copy.202
  199.5 0.1 copy.211
  199.7 0.2 fusion.15
  199.9 0.1 broadcast_in_dim.166
  200.1 14.9 %all_to_all.15 = bf16[32,8,2,2,128]{4,3,2,1,0:T(2,128)(2,1)S(1)} all-to-all(bf16[32,8,2,2,128]{4,3,2,1,0:T(2,128)(2,1)S(1)} %broadcast_in_dim.166), channel_id=1, replica_groups=mesh['group'=8,'tp'=32] {'tp'}, dimensions={0} | all-to-all | bytes 524288 | tf_op jit(solution)/shard_map/all_to_all | solution.py:30
  215.0 0.2 copy.213
  215.2 0.2 reshape_reshape.3
  215.4 2.8 %convolution_convert_fusion = bf16[16,256]{1,0:T(8,128)(2,1)S(1)} fusion(bf16[16,8192]{1,0:T(8,128)(2,1)S(1)} %reshape_reshape.3, bf16[8192,256]{1,0:T(8,128)(2,1)} %param.21), kind=kOutput, calls=%fused_computation.30 | convolution fusion | flops 67112960 | bytes 4464640 | tf_op jit(solution)/shard_map/dot_general | solution.py:229
  218.3 0.6 reshape.270
  (64 shorter events, 2.8 us)
Async XLA Ops:
  0.0 111.1 %collective-permute-start = (s32[8]{0:T(128)}, s32[8]{0:T(128)S(1)}, u32[]{:S(2)}, u32[]{:S(2)}) collective-permute-start(s32[8]{0:T(128)} %bitcast.157), channel_id=1, source_target_pairs={{0,128},{32,160},{64,192},{96,224},{128,0},{160,32},{192,64},{224,... | collective-permute-start | bytes 104 | tf_op jit(solution)/shard_map/ppermute | solution.py:25
  66.2 2.4 %copy-start.1 = (bf16[1,64,16,1024]{3,2,1,0:T(8,128)(2,1)S(1)}, bf16[1,64,16,1024]{3,2,1,0:T(8,128)(2,1)}, u32[]{:S(2)}) copy-start(bf16[1,64,16,1024]{3,2,1,0:T(8,128)(2,1)} %param.17) | copy-start | bytes 6291460
  69.2 1.5 copy-start.4
  69.2 1.6 copy-start.5
  69.2 41.8 %copy-start.6 = (s32[1,64]{1,0:T(1,128)S(1)}, s32[1,64]{1,0:T(1,128)}, u32[]{:S(2)}) copy-start(s32[1,64]{1,0:T(1,128)} %param.19) | copy-start | bytes 772
  114.5 4.4 %collective-permute-start.1 = (bf16[1,2,8192]{2,1,0:T(2,128)(2,1)S(1)}, bf16[1,2,8192]{2,1,0:T(2,128)(2,1)S(1)}, u32[]{:S(2)}, u32[]{:S(2)}) collective-permute-start(bf16[1,2,8192]{2,1,0:T(2,128)(2,1)S(1)} %copy.277), channel_id=1, source_target_pairs={{0,128},{32,160},{64,192},{96,224},{128,0},{160,32},{192,64},{224,... | collective-permute-start | bytes 98312 | tf_op jit(solution)/shard_map/ppermute | solution.py:25
  133.9 7.9 %copy-start.2 = (bf16[64,16,8,128,1]{3,2,1,0,4:T(8,128)(2,1)S(1)}, bf16[64,16,8,128,1]{3,2,1,0,4:T(8,128)(2,1)}, u32[]{:S(2)}) copy-start(bf16[64,16,8,128,1]{3,2,1,0,4:T(8,128)(2,1)} %bitcast_bitcast_fusion) | copy-start | bytes 6291460
  135.2 10.8 %collective-permute-start.2 = (f32[1,2,64]{2,1,0:T(2,128)S(1)}, f32[1,2,64]{2,1,0:T(2,128)S(1)}, u32[]{:S(2)}, u32[]{:S(2)}) collective-permute-start(f32[1,2,64]{2,1,0:T(2,128)S(1)} %slice.47), channel_id=1, source_target_pairs={{0,128},{32,160},{64,192},{96,224},{128,0},{160,32},{192,64},{224,... | collective-permute-start | bytes 1544 | tf_op jit(solution)/shard_map/ppermute | solution.py:25
  136.1 5.7 %copy-start = (f32[64,8,2,8,16]{4,3,2,1,0:T(8,128)S(1)}, f32[64,8,2,8,16]{4,3,2,1,0:T(8,128)}, u32[]{:S(2)}) copy-start(f32[64,8,2,8,16]{4,3,2,1,0:T(8,128)} %get-tuple-element.41) | copy-start | bytes 1572868
  144.3 1.4 copy-start.3
  146.9 13.9 %all-to-all-start = ((f32[32,1,1024]{2,1,0:T(1,128)}), f32[32,1,1024]{2,1,0:T(1,128)S(1)}, u32[]{:S(2)}, u32[]{:S(2)}) async-start(f32[32,1,1024]{2,1,0:T(1,128)} %reshape.380), calls=%async_computation | async-start | bytes 262144 | tf_op jit(solution)/shard_map/all_to_all | solution.py:30
  152.4 10.1 %collective-permute-start.3 = (f32[1,2,64]{2,1,0:T(2,128)S(1)}, f32[1,2,64]{2,1,0:T(2,128)S(1)}, u32[]{:S(2)}, u32[]{:S(2)}) collective-permute-start(f32[1,2,64]{2,1,0:T(2,128)S(1)} %slice.49), channel_id=1, source_target_pairs={{0,128},{32,160},{64,192},{96,224},{128,0},{160,32},{192,64},{224,... | collective-permute-start | bytes 1544 | tf_op jit(solution)/shard_map/ppermute | solution.py:25
  155.2 8.5 %collective-permute-start.4 = (f32[1,2,64,128]{3,2,1,0:T(8,128)S(1)}, f32[1,2,64,128]{3,2,1,0:T(8,128)S(1)}, u32[]{:S(2)}, u32[]{:S(2)}) collective-permute-start(f32[1,2,64,128]{3,2,1,0:T(8,128)S(1)} %bitcast.156), channel_id=1, source_target_pairs={{0,128},{32,160},{64,192},{96,224},{128,0},{160,32},{192,64},{224,... | collective-permute-start | bytes 196616 | tf_op jit(solution)/shard_map/ppermute | solution.py:25
  165.7 33.2 %all-to-all-start.1 = ((f32[32,8,2,2,129]{4,1,3,2,0:T(8,128)}), f32[32,8,2,2,129]{4,1,3,2,0:T(8,128)S(1)}, u32[]{:S(2)}, u32[]{:S(2)}) async-start(f32[32,8,2,2,129]{4,1,3,2,0:T(8,128)} %copy.193), calls=%async_computation.1 | async-start | bytes 2097152 | tf_op jit(solution)/shard_map/all_to_all | solution.py:46
where the time goes:
time: 220 us; the launch traced here: 219 us
  blocking collectives  101 us (46%)
  waiting for transfers between devices  32.8 us (15%)
  local copies, waits for them, and re-layouts  29.4 us (13%)
  other arithmetic  24.5 us (11%)
  starting transfers between devices  17.6 us (8%)
  matrix products  12.8 us (6%)
    all_gather x1, blocking collectives, per_device(): lax.all_gather(queries[0], 'tp', axis=2, tiled=True)  46.4 us
    all_gather x1, blocking collectives, side_by_side(): lax.all_gather(both, axis, axis=dim, tiled=True)  40.1 us
    all_to_all x1, waiting for transfers between devices, summed_on_arrival(): lax.all_to_all(blocks, axis, split_axis=0, concat_axis=0, tiled=True)  24.4 us
    all_to_all x1, blocking collectives, copy_for_each(): lax.all_to_all(jnp.broadcast_to(value[None], (peers, *value.shape)), axis...  14.9 us
    lt x1, other arithmetic, page_states(): owner_rows < row_count  10.6 us
    gather x2, local copies, waits for them, and re-layouts, page_states(): jnp.take(query_rows, clipped, axis=0)  8.91 us
    ppermute x5, starting transfers between devices, swapped(): lax.ppermute(value, axis, [(i, i ^ 1 << distance) for i in range(lax.axis...  7.21 us
    dot_general x1, matrix products, page_states(): jnp.einsum('psgjd,ptgd->psgjt', query_page, key_page, preferred_element_t...  5.79 us
  transfers between devices with their start and end apart: 7, of which 3 were waited for; matrix products, arithmetic and copies ran while one was open for 17% of the time, Pallas kernels for 0%

commit v1 on v0

--- a/solution.py
+++ b/solution.py
@@ -159,7 +159,9 @@
     step_count = queries.shape[2]
     partner_bit = lax.axis_size("group").bit_length() - 2
     query_rows, key_rows, value_rows = (
-        lax.all_gather(queries[0], "tp", axis=2, tiled=True),
+        jnp.concatenate(
+            lax.all_to_all(jnp.stack([queries[0]] * lax.axis_size("tp")), "tp", 0, 0), axis=2
+        ),
         *side_by_side((new_keys[0], new_values[0]), "tp", 2, 0),
     )
     owners = page_owner[0]

time: 220 us -> 193 us (0.88)
  blocking collectives: 101 us -> 60.5 us
  starting transfers between devices: 17.6 us -> 27.1 us
  local copies, waits for them, and re-layouts: 29.4 us -> 32.4 us
    all_gather x1 -> x0, blocking collectives: 46.4 us -> none  [per_device(): lax.all_gather(queries[0], 'tp', axis=2, tiled=True)]
    all_to_all x0 -> x1, starting transfers between devices: none -> 9.47 us  [per_device(): lax.all_to_all(jnp.stack([queries[0]] * lax.axis_size('tp')), 'tp', 0, 0)]
    all_gather x1, blocking collectives: 40.1 us -> 45.6 us  [side_by_side(): lax.all_gather(both, axis, axis=dim, tiled=True)]
    unnamed x21 -> x23, local copies, waits for them, and re-layouts: 4.86 us -> 4.86 us
  transfers between devices with their start and end apart: 7 -> 8, of which waited for: 3 -> 3; matrix products, arithmetic and copies ran while one was open for 17% -> 23% of each run, Pallas kernels for 0% -> 0%
where the time goes in v1:
time: 193 us; the launch traced here: 192 us
  blocking collectives  60.5 us (31%)
  waiting for transfers between devices  33.3 us (17%)
  local copies, waits for them, and re-layouts  32.4 us (17%)
  starting transfers between devices  27.1 us (14%)
  other arithmetic  24.3 us (13%)
  matrix products  13.8 us (7%)
    all_gather x1, blocking collectives, side_by_side(): lax.all_gather(both, axis, axis=dim, tiled=True)  45.6 us
    all_to_all x1, waiting for transfers between devices, summed_on_arrival(): lax.all_to_all(blocks, axis, split_axis=0, concat_axis=0, tiled=True)  25.1 us
    all_to_all x1, blocking collectives, copy_for_each(): lax.all_to_all(jnp.broadcast_to(value[None], (peers, *value.shape)), axis...  14.9 us
    lt x1, other arithmetic, page_states(): owner_rows < row_count  10.6 us
    all_to_all x1, starting transfers between devices, per_device(): lax.all_to_all(jnp.stack([queries[0]] * lax.axis_size('tp')), 'tp', 0, 0)  9.47 us
    gather x2, local copies, waits for them, and re-layouts, page_states(): jnp.take(query_rows, clipped, axis=0)  8.91 us
    ppermute x5, starting transfers between devices, swapped(): lax.ppermute(value, axis, [(i, i ^ 1 << distance) for i in range(lax.axis...  7.41 us
    dot_general x1, matrix products, page_states(): jnp.einsum('psgjd,ptgd->psgjt', query_page, key_page, preferred_element_t...  5.73 us
  transfers between devices with their start and end apart: 8, of which 3 were waited for; matrix products, arithmetic and copies ran while one was open for 23% of the time, Pallas kernels for 0%

profile of v1, /device:TPU:1, one launch (start us, length us, event | category | flops | bytes accessed | tf_op | source)
XLA Modules:
  0.0 191.9 jit_solution(15538681211634432526)
XLA Ops:
  0.0 3.7 %collective-permute-start = (s32[8]{0:T(128)}, s32[8]{0:T(128)S(1)}, u32[]{:S(2)}, u32[]{:S(2)}) collective-permute-start(s32[8]{0:T(128)} %bitcast.164), channel_id=1, source_target_pairs={{0,128},{32,160},{64,192},{96,224},{128,0},{160,32},{192,64},{224,... | collective-permute-start | bytes 104 | tf_op jit(solution)/shard_map/ppermute | solution.py:25
  3.7 1.5 stack.3
  5.3 9.5 %all-to-all-start = ((bf16[32,8,2,256]{3,2,1,0:T(2,128)(2,1)}), bf16[32,8,2,256]{3,2,1,0:T(2,128)(2,1)S(1)}, u32[]{:S(2)}, u32[]{:S(2)}) async-start(bf16[32,8,2,256]{3,2,1,0:T(2,128)(2,1)} %stack.3), calls=%async_computation | async-start | bytes 524288 | tf_op jit(solution)/shard_map/all_to_all | solution.py:163
  14.8 1.6 fusion.43
  16.4 0.7 fusion.35
  17.0 0.2 reduce-window.18
  17.2 0.7 fusion.44
  17.9 10.6 %broadcast_compare_fusion = (pred[64]{0:T(512)(128)(4,1)S(1)}, s32[64]{0:T(128)S(1)}) fusion(s32[]{:T(128)} %bitcast.19, s32[]{:T(128)} %bitcast.18, s32[]{:T(128)} %bitcast.17, s32[]{:T(128)} %bitcast.16, s32[]{:T(128)} %bitcast.15, s32[]{:T(128)} %bitcast.14, s32[]{:T(128)} %bitcast.13, s32[]{:T(128)} %bitcast.12, s32[]{:T(128)} %bitcast.9, s32[]{:T(128)} %bitcast.8, ...), kind=kLoop, calls=%fused_computation.114 | loop fusion | flops 2368 | bytes 640 | tf_op jit(solution)/shard_map/lt | solution.py:97
  28.6 2.2 %copy.256 = bf16[128,8,8,128]{3,2,1,0:T(8,128)(2,1)S(1)} copy(bf16[128,8,8,128]{3,1,2,0:T(8,128)(2,1)} %bitcast.150) | data formatting | bytes 4194304
  30.8 1.5 bitcast_bitcast_fusion.1
  32.3 0.9 copy-done.1
  33.1 0.6 copy.257
  33.8 1.5 bitcast_bitcast_fusion
  35.6 45.6 %all_gather.3 = bf16[16,2,1024]{0,1,2:T(2,128)(2,1)S(1)} all-gather(bf16[16,2,32]{0,1,2:T(2,128)(2,1)S(1)} %pad_maximum_fusion.1), channel_id=1, replica_groups=mesh['group'=8,'tp'=32] {'tp'}, dimensions={2}, use_global_device_ids=true | all-gather | bytes 67584 | tf_op jit(solution)/shard_map/all_gather | solution.py:21
  81.2 1.8 fusion.42
  83.0 0.2 reduce-window.19
  83.2 0.6 fusion.38
  83.9 0.6 select_reduce_fusion.1
  84.5 1.3 bitcast_convert_fusion.1
  86.0 1.5 fusion.30
  87.6 0.1 collective-permute-start.1
  87.7 1.3 compare_and_fusion.2
  89.0 0.3 copy.197
  89.3 2.7 %collective-permute-done.1 = bf16[1,2,8192]{2,1,0:T(2,128)(2,1)S(1)} collective-permute-done((bf16[1,2,8192]{2,1,0:T(2,128)(2,1)S(1)}, bf16[1,2,8192]{2,1,0:T(2,128)(2,1)S(1)}, u32[]{:S(2)}, u32[]{:S(2)}) %collective-permute-start.1) | collective-permute-done | bytes 32800 | tf_op jit(solution)/shard_map/ppermute | solution.py:25
  91.9 0.4 pad_maximum_fusion
  92.3 6.0 %gather_fusion = bf16[64,2,8192]{2,1,0:T(2,128)(2,1)S(1)} fusion(bf16[9,2,8192]{2,1,0:T(2,128)(2,1)S(1)} %pad_maximum_fusion, s32[1024]{0:T(1024)S(1)} %pad_clamp_fusion.1), kind=kCustom, calls=%fused_computation.2 | custom fusion | bytes 4194560 | tf_op jit(solution)/shard_map/jit(_take)/gather | solution.py:88
  98.4 2.9 %reshape.369 = bf16[64,2,8,8,128]{4,3,2,1,0:T(8,128)(2,1)} reshape(bf16[64,2,8192]{2,1,0:T(2,128)(2,1)S(1)} %gather_fusion) | data formatting | bytes 4194304 | tf_op jit(solution)/shard_map/jit(_take)/gather | solution.py:88
  101.2 5.7 %bitcast_reduce_fusion = (f32[64,2,8,8]{3,1,2,0:T(2,128)S(1)}, f32[64,8,2,8,16]{4,3,2,1,0:T(8,128)}) fusion(pred[64,16]{1,0:T(8,128)(4,1)S(1)} %fusion.17, bf16[64,16,8,128,1]{3,2,1,0,4:T(8,128)(2,1)} %bitcast_bitcast_fusion.1, bf16[64,2,8,8,128]{4,3,2,1,0:T(8,128)(2,1)} %reshape.369, pred[64]{0:T(512)(128)(4,1)S(1)} %get-tuple-element.18), kind=kOutput, calls=%fused_computation.8 | convolution fusion | flops 34988032 | bytes 4752448 | tf_op jit(solution)/shard_map/psgjd,ptgd->psgjt/dot_general | solution.py:94
  107.0 0.3 copy.201
  107.3 0.2 select_reduce_fusion
  107.5 0.6 gather_fusion.1
  108.2 0.6 collective-permute-start.2
  108.9 0.4 copy.204
  109.3 5.7 %convert_reduce_fusion = bf16[64,2,8,8]{3,1,2,0:T(2,128)(2,1)} fusion(f32[64,2,8,8]{3,1,2,0:T(2,128)S(1)} %copy.204, f32[64,8,2,8,16]{4,3,2,1,0:T(8,128)} %get-tuple-element.41, pred[64,16]{1,0:T(8,128)(4,1)S(1)} %fusion.17), kind=kLoop, calls=%fused_computation.12 | loop fusion | flops 909312 | bytes 574464 | tf_op jit(solution)/shard_map/reduce_sum | solution.py:112
  115.1 2.0 %convolution_bitcast_fusion = bf16[64,2,8,8,128]{4,3,1,2,0:T(8,128)(2,1)S(1)} fusion(bf16[64,16,8,128,1]{3,2,1,0,4:T(8,128)(2,1)S(1)} %copy-done.2, f32[64,8,2,8,16]{4,3,2,1,0:T(8,128)S(1)} %copy-done, f32[64,2,8,8]{3,1,2,0:T(2,128)S(1)} %copy.204, pred[64,16]{1,0:T(8,128)(4,1)S(1)} %fusion.17), kind=kOutput, calls=%fused_computation.14 | convolution fusion | flops 34209792 | bytes 4752384 | tf_op jit(solution)/shard_map/psgjt,ptgd->psgjd/dot_general | solution.py:109
  117.1 0.5 copy.211
  117.6 1.2 fusion
  119.0 0.2 copy.205
  119.3 0.8 reshape.382
  120.2 4.9 %all-to-all-start.1 = ((f32[32,1,1024]{2,1,0:T(1,128)}), f32[32,1,1024]{2,1,0:T(1,128)S(1)}, u32[]{:S(2)}, u32[]{:S(2)}) async-start(f32[32,1,1024]{2,1,0:T(1,128)} %reshape.382), calls=%async_computation.1 | async-start | bytes 262144 | tf_op jit(solution)/shard_map/all_to_all | solution.py:30
  125.4 2.9 %collective-permute-start.3 = (f32[1,2,64]{2,1,0:T(2,128)S(1)}, f32[1,2,64]{2,1,0:T(2,128)S(1)}, u32[]{:S(2)}, u32[]{:S(2)}) collective-permute-start(f32[1,2,64]{2,1,0:T(2,128)S(1)} %slice.49), channel_id=1, source_target_pairs={{0,128},{32,160},{64,192},{96,224},{128,0},{160,32},{192,64},{224,... | collective-permute-start | bytes 1544 | tf_op jit(solution)/shard_map/ppermute | solution.py:25
  128.4 5.5 %all-to-all-done.1 = f32[32,1,1024]{2,1,0:T(1,128)S(1)} async-done(((f32[32,1,1024]{2,1,0:T(1,128)}), f32[32,1,1024]{2,1,0:T(1,128)S(1)}, u32[]{:S(2)}, u32[]{:S(2)}) %all-to-all-start.1) | async-done | bytes 131104 | tf_op jit(solution)/shard_map/all_to_all | solution.py:30
  133.9 0.5 broadcast.381
  134.4 0.9 reduce.12
  136.0 0.8 copy.215
  136.8 0.5 add_multiply_fusion
  137.3 0.3 maximum_bitcast_fusion
  137.6 1.1 copy.216
  138.7 5.3 %all-to-all-start.2 = ((f32[32,8,2,2,129]{4,1,3,2,0:T(8,128)}), f32[32,8,2,2,129]{4,1,3,2,0:T(8,128)S(1)}, u32[]{:S(2)}, u32[]{:S(2)}) async-start(f32[32,8,2,2,129]{4,1,3,2,0:T(8,128)} %copy.216), calls=%async_computation.2 | async-start | bytes 2097152 | tf_op jit(solution)/shard_map/all_to_all | solution.py:46
  144.1 0.3 copy.222
  144.4 0.3 copy.229
  144.8 0.6 gather_fusion.2
  145.4 0.6 gather_fusion.3
  146.2 0.2 fusion.45
  146.7 25.1 %all-to-all-done.2 = f32[32,8,2,2,129]{4,1,3,2,0:T(8,128)S(1)} async-done(((f32[32,8,2,2,129]{4,1,3,2,0:T(8,128)}), f32[32,8,2,2,129]{4,1,3,2,0:T(8,128)S(1)}, u32[]{:S(2)}, u32[]{:S(2)}) %all-to-all-start.2) | async-done | bytes 528416 | tf_op jit(solution)/shard_map/all_to_all | solution.py:46
  172.0 0.2 copy.252
  172.3 0.1 copy.227
  172.7 0.2 fusion.15
  173.0 0.1 broadcast_in_dim.166
  173.1 14.9 %all_to_all.20 = bf16[32,8,2,2,128]{4,3,2,1,0:T(2,128)(2,1)S(1)} all-to-all(bf16[32,8,2,2,128]{4,3,2,1,0:T(2,128)(2,1)S(1)} %broadcast_in_dim.166), channel_id=1, replica_groups=mesh['group'=8,'tp'=32] {'tp'}, dimensions={0} | all-to-all | bytes 524288 | tf_op jit(solution)/shard_map/all_to_all | solution.py:30
  188.0 0.2 copy.238
  188.3 0.2 reshape_reshape.7
  188.5 2.8 %convolution_convert_fusion = bf16[16,256]{1,0:T(8,128)(2,1)S(1)} fusion(bf16[16,8192]{1,0:T(8,128)(2,1)S(1)} %reshape_reshape.7, bf16[8192,256]{1,0:T(8,128)(2,1)} %param.21), kind=kOutput, calls=%fused_computation.30 | convolution fusion | flops 67112960 | bytes 4464640 | tf_op jit(solution)/shard_map/dot_general | solution.py:231
  191.3 0.6 reshape.274
  (74 shorter events, 3.5 us)
Async XLA Ops:
  0.0 83.0 %collective-permute-start = (s32[8]{0:T(128)}, s32[8]{0:T(128)S(1)}, u32[]{:S(2)}, u32[]{:S(2)}) collective-permute-start(s32[8]{0:T(128)} %bitcast.164), channel_id=1, source_target_pairs={{0,128},{32,160},{64,192},{96,224},{128,0},{160,32},{192,64},{224,... | collective-permute-start | bytes 104 | tf_op jit(solution)/shard_map/ppermute | solution.py:25
  5.3 80.5 %all-to-all-start = ((bf16[32,8,2,256]{3,2,1,0:T(2,128)(2,1)}), bf16[32,8,2,256]{3,2,1,0:T(2,128)(2,1)S(1)}, u32[]{:S(2)}, u32[]{:S(2)}) async-start(bf16[32,8,2,256]{3,2,1,0:T(2,128)(2,1)} %stack.3), calls=%async_computation | async-start | bytes 524288 | tf_op jit(solution)/shard_map/all_to_all | solution.py:163
  30.8 2.4 %copy-start.1 = (bf16[1,64,16,1024]{3,2,1,0:T(8,128)(2,1)S(1)}, bf16[1,64,16,1024]{3,2,1,0:T(8,128)(2,1)}, u32[]{:S(2)}) copy-start(bf16[1,64,16,1024]{3,2,1,0:T(8,128)(2,1)} %param.17) | copy-start | bytes 6291460
  33.8 1.5 copy-start.5
  33.8 1.6 copy-start.6
  35.3 47.7 %copy-start.7 = (s32[1,64]{1,0:T(1,128)S(1)}, s32[1,64]{1,0:T(1,128)}, u32[]{:S(2)}) copy-start(s32[1,64]{1,0:T(1,128)} %param.19) | copy-start | bytes 772
  87.6 4.4 %collective-permute-start.1 = (bf16[1,2,8192]{2,1,0:T(2,128)(2,1)S(1)}, bf16[1,2,8192]{2,1,0:T(2,128)(2,1)S(1)}, u32[]{:S(2)}, u32[]{:S(2)}) collective-permute-start(bf16[1,2,8192]{2,1,0:T(2,128)(2,1)S(1)} %copy.308), channel_id=1, source_target_pairs={{0,128},{32,160},{64,192},{96,224},{128,0},{160,32},{192,64},{224,... | collective-permute-start | bytes 98312 | tf_op jit(solution)/shard_map/ppermute | solution.py:25
  107.0 8.1 %copy-start.2 = (bf16[64,16,8,128,1]{3,2,1,0,4:T(8,128)(2,1)S(1)}, bf16[64,16,8,128,1]{3,2,1,0,4:T(8,128)(2,1)}, u32[]{:S(2)}) copy-start(bf16[64,16,8,128,1]{3,2,1,0,4:T(8,128)(2,1)} %bitcast_bitcast_fusion) | copy-start | bytes 6291460
  108.2 11.0 %collective-permute-start.2 = (f32[1,2,64]{2,1,0:T(2,128)S(1)}, f32[1,2,64]{2,1,0:T(2,128)S(1)}, u32[]{:S(2)}, u32[]{:S(2)}) collective-permute-start(f32[1,2,64]{2,1,0:T(2,128)S(1)} %slice.47), channel_id=1, source_target_pairs={{0,128},{32,160},{64,192},{96,224},{128,0},{160,32},{192,64},{224,... | collective-permute-start | bytes 1544 | tf_op jit(solution)/shard_map/ppermute | solution.py:25
  109.3 5.7 %copy-start = (f32[64,8,2,8,16]{4,3,2,1,0:T(8,128)S(1)}, f32[64,8,2,8,16]{4,3,2,1,0:T(8,128)}, u32[]{:S(2)}) copy-start(f32[64,8,2,8,16]{4,3,2,1,0:T(8,128)} %get-tuple-element.41) | copy-start | bytes 1572868
  117.6 1.4 copy-start.4
  120.2 13.7 %all-to-all-start.1 = ((f32[32,1,1024]{2,1,0:T(1,128)}), f32[32,1,1024]{2,1,0:T(1,128)S(1)}, u32[]{:S(2)}, u32[]{:S(2)}) async-start(f32[32,1,1024]{2,1,0:T(1,128)} %reshape.382), calls=%async_computation.1 | async-start | bytes 262144 | tf_op jit(solution)/shard_map/all_to_all | solution.py:30
  125.4 10.1 %collective-permute-start.3 = (f32[1,2,64]{2,1,0:T(2,128)S(1)}, f32[1,2,64]{2,1,0:T(2,128)S(1)}, u32[]{:S(2)}, u32[]{:S(2)}) collective-permute-start(f32[1,2,64]{2,1,0:T(2,128)S(1)} %slice.49), channel_id=1, source_target_pairs={{0,128},{32,160},{64,192},{96,224},{128,0},{160,32},{192,64},{224,... | collective-permute-start | bytes 1544 | tf_op jit(solution)/shard_map/ppermute | solution.py:25
  128.3 8.5 %collective-permute-start.4 = (f32[1,2,64,128]{3,2,1,0:T(8,128)S(1)}, f32[1,2,64,128]{3,2,1,0:T(8,128)S(1)}, u32[]{:S(2)}, u32[]{:S(2)}) collective-permute-start(f32[1,2,64,128]{3,2,1,0:T(8,128)S(1)} %bitcast.163), channel_id=1, source_target_pairs={{0,128},{32,160},{64,192},{96,224},{128,0},{160,32},{192,64},{224,... | collective-permute-start | bytes 196616 | tf_op jit(solution)/shard_map/ppermute | solution.py:25
  137.6 6.4 %copy-start.3 = (bf16[8,2,1024]{0,1,2:T(2,128)(2,1)S(1)}, bf16[8,2,1024]{0,1,2:T(2,128)(2,1)}, u32[]{:S(2)}) copy-start(bf16[8,2,1024]{0,1,2:T(2,128)(2,1)} %get-tuple-element.21) | copy-start | bytes 98308
  138.7 33.2 %all-to-all-start.2 = ((f32[32,8,2,2,129]{4,1,3,2,0:T(8,128)}), f32[32,8,2,2,129]{4,1,3,2,0:T(8,128)S(1)}, u32[]{:S(2)}, u32[]{:S(2)}) async-start(f32[32,8,2,2,129]{4,1,3,2,0:T(8,128)} %copy.216), calls=%async_computation.2 | async-start | bytes 2097152 | tf_op jit(solution)/shard_map/all_to_all | solution.py:46
